TPU v7x, 256 devices: a whole 4x4x8 slice. The times are simulated.
256 devices in a mesh: shot: 2 (over x_lo), space: 128 (over z, x_hi, y, core).
Axes of the slice: x: 4 (x_hi: 2, x_lo: 2; x = x_hi * 2 + x_lo), y: 4, z: 8, core: 2. Of those that a mesh axis runs over, the one named last changes fastest.
Arguments:
- pressure_now: float32 [4, 128, 4, 128, 128], P('shot', 'space'), may hold values from -6 to 6
- pressure_old: float32 [4, 128, 4, 128, 128], P('shot', 'space'), may hold values from -6 to 6
- auxiliary_now: float32 [4, 128, 4, 128, 128], P('shot', 'space'), may hold values from -6 to 6
- auxiliary_old: float32 [4, 128, 4, 128, 128], P('shot', 'space'), may hold values from -6 to 6
- velocity: float32 [128, 4, 128, 128], P('space', 'shot'), may hold values from 1.5 to 4
- epsilon_field: float32 [128, 4, 128, 128], P('space', 'shot'), may hold values from 0.1 to 0.3
- delta_field: float32 [128, 4, 128, 128], P('space', 'shot'), may hold values from 0 to 0.1
- active_blocks: int32 [4, 128], P('shot', 'space'), may hold values 0 or 1
- source_cells: int32 [4], P('shot'), may hold values from 0 to 8388607
- receiver_cells: int32 [4, 256], P('shot'), may hold values from 0 to 8388607
- wavelet: float32 [4, 4], P('shot'), may hold values from -4 to 4
Outputs:
- pressure_final: float32 [4, 128, 4, 128, 128], P('shot', 'space')
- auxiliary_final: float32 [4, 128, 4, 128, 128], P('shot', 'space')
- traces: float32 [4, 4, 256], P('shot')
Inputs may be any that keep to these rules, and one draw needn't show every extreme that they name: `source_cells`: cell numbers of the aperture. `receiver_cells`: cell numbers of the aperture.
All inputs are finite; a program needn't handle non-finite values. No bound on the sum of `active_blocks` on one device may be relied on, other than what follows from the above.
Results may differ from a plain program's by a relative error of at most 0.00002.
Values sent between devices are 32-bit elements; how exact they have to be, the bound alone decides.
No kernel may reach another device: no remote copies, remote signals or barrier semaphores. Data moves between devices by JAX's collectives and lax.ppermute only.
A program may use at most 64 MiB of HBM per device.

v0:
```python
import jax
import jax.numpy as jnp
from jax import lax
from jax.sharding import PartitionSpec as P

STEPS = 4
stencil_taps = (-205.0 / 72.0, 8.0 / 5.0, -1.0 / 5.0, 8.0 / 315.0, -1.0 / 560.0)
step_ratio = 0.08


def passed_along(value, axis, by):
    count = lax.axis_size(axis)
    pairs = [(i, i + by) for i in range(count) if 0 <= i + by < count]
    return lax.ppermute(value, axis, pairs)


def second_diff(padded, along, length):

    def window(offset):
        return lax.slice_in_dim(padded, 4 + offset, 4 + offset + length, axis=along)

    summed = stencil_taps[0] * window(0)
    for offset in range(1, 5):
        summed = summed + stencil_taps[offset] * (window(offset) + window(-offset))
    return summed


def padded_fields(pressure, auxiliary):
    lower_x = passed_along(pressure, "space", 1)
    upper_x = passed_along(pressure, "space", -1)
    padded_x = jnp.concatenate([lower_x, pressure, upper_x], axis=1)
    padded_y = jnp.pad(pressure, ((0, 0), (0, 0), (4, 4), (0, 0)))
    padded_z = jnp.pad(auxiliary, ((0, 0), (0, 0), (0, 0), (4, 4)))
    return (padded_x, padded_y, padded_z)


def advance(state, padded, medium, source_local, source_gain, live_mask):
    pressure, pressure_prev, auxiliary, auxiliary_prev = state
    padded_x, padded_y, padded_z = padded
    courant, stretch, coupling = medium
    horizontal = second_diff(padded_x, 1, pressure.shape[1]) + second_diff(
        padded_y, 2, pressure.shape[2]
    )
    vertical = second_diff(padded_z, 3, auxiliary.shape[3])
    new_p = 2.0 * pressure - pressure_prev + courant * (stretch * horizontal + coupling * vertical)
    new_q = 2.0 * auxiliary - auxiliary_prev + courant * (coupling * horizontal + vertical)
    count = pressure.shape[0]
    shape_now = pressure.shape
    rows = jnp.arange(count, dtype=jnp.int32)
    new_p = new_p.reshape(count, -1).at[rows, source_local].add(source_gain).reshape(shape_now)
    new_q = new_q.reshape(count, -1).at[rows, source_local].add(source_gain).reshape(shape_now)
    gains = live_mask[:, None, None, None]
    return (new_p * gains, new_q * gains)


def per_device(
    pressure_now,
    pressure_old,
    auxiliary_now,
    auxiliary_old,
    velocity,
    epsilon_field,
    delta_field,
    active_blocks,
    source_cells,
    receiver_cells,
    wavelet,
):
    shots = pressure_now.shape[0]
    rows_x, rows_y, rows_z = (pressure_now.shape[2], pressure_now.shape[3], pressure_now.shape[4])
    cells = rows_x * rows_y * rows_z
    position = lax.axis_index("space")
    speed, aniso_eps, aniso_delta = (
        lax.all_gather(velocity, "shot", axis=1, tiled=True),
        lax.all_gather(epsilon_field, "shot", axis=1, tiled=True),
        lax.all_gather(delta_field, "shot", axis=1, tiled=True),
    )
    courant = (speed[0] * step_ratio) ** 2
    stretch = 1.0 + 2.0 * aniso_eps[0]
    coupling = jnp.sqrt(1.0 + 2.0 * aniso_delta[0])
    medium = (courant, stretch, coupling)
    source_block = source_cells // cells
    source_here = (source_block == position).astype(jnp.float32)
    live_all = jnp.maximum(
        active_blocks[:, 0], (source_block == position).astype(jnp.int32)
    ).astype(jnp.float32)
    source_local = source_cells % cells
    receiver_here = (receiver_cells // cells == position).astype(jnp.float32)
    receiver_local = receiver_cells % cells
    fields = [
        member.reshape(shots, rows_x, rows_y, rows_z) * live_all[:, None, None, None]
        for member in (pressure_now, pressure_old, auxiliary_now, auxiliary_old)
    ]
    groups = [(0, shots)]
    states = [tuple((member for member in fields)) for start, stop in groups]
    recorded = [[] for start, stop in groups]
    for time_step in range(STEPS):
        start, stop = groups[0]
        state = states[0]
        padded = padded_fields(state[0], state[2])
        gains_now = wavelet[start:stop, time_step] * source_here
        new_p, new_q = advance(state, padded, medium, source_local, gains_now, live_all)
        sampled = jnp.take_along_axis(new_p.reshape(stop - start, cells), receiver_local, axis=1)
        recorded[0].append(sampled * receiver_here)
        states[0] = (new_p, state[0], new_q, state[2])
    local_traces = jnp.concatenate([jnp.stack(samples, axis=1) for samples in recorded], axis=0)
    traces = lax.psum(local_traces, "space")
    pressure_final = jnp.concatenate([state[0] for state in states], axis=0).reshape(
        shots, 1, rows_x, rows_y, rows_z
    )
    auxiliary_final = jnp.concatenate([state[2] for state in states], axis=0).reshape(
        shots, 1, rows_x, rows_y, rows_z
    )
    return (pressure_final, auxiliary_final, traces)


def solution(mesh):
    return jax.shard_map(
        per_device,
        mesh=mesh,
        in_specs=(
            P("shot", "space", None, None, None),
            P("shot", "space", None, None, None),
            P("shot", "space", None, None, None),
            P("shot", "space", None, None, None),
            P("space", "shot", None, None),
            P("space", "shot", None, None),
            P("space", "shot", None, None),
            P("shot", "space"),
            P("shot"),
            P("shot", None),
            P("shot", None),
        ),
        out_specs=(
            P("shot", "space", None, None, None),
            P("shot", "space", None, None, None),
            P("shot", None, None),
        ),
        check_vma=False,
    )
```

profile of v0, /device:TPU:128, one launch (start us, length us, event | category | flops | bytes accessed | tf_op | source)
XLA Modules:
  0.0 473.6 jit_solution(8549668667365122625)
XLA Ops:
  0.6 0.7 copy-done.13
  1.5 0.6 copy-done.15
  2.2 0.6 copy-done.16
  2.9 1.4 bitcast_multiply_fusion.3
  4.3 6.4 %collective-permute-start = (f32[2,4,128,128]{3,2,1,0:T(8,128)S(1)}, f32[2,4,128,128]{3,2,1,0:T(8,128)S(1)}, u32[]{:S(2)}, u32[]{:S(2)}) collective-permute-start(f32[2,4,128,128]{3,2,1,0:T(8,128)S(1)} %get-tuple-element.52), channel_id=1, source_target_pairs={{1,0},{2,1},{3,2},{4,3},{5,4},{6,5},{7,6},{8,7},{9,8},{10,9},{11,1... | collective-permute-start | bytes 1572872 | tf_op jit(solution)/shard_map/ppermute | solution.py:14
  10.7 1.9 collective-permute-start.1
  12.6 8.9 %all_gather.9 = f32[1,4,128,128]{3,2,0,1:T(8,128)S(1)} all-gather(f32[1,2,128,128]{3,2,0,1:T(8,128)S(1)} %bitcast.155), channel_id=1, replica_groups=mesh['shot'=2,'space'=128] {'shot'}, dimensions={1}, use_global_device_ids=true | all-gather | bytes 393216 | tf_op jit(solution)/shard_map/all_gather | solution.py:74
  21.6 0.9 copy-done.11
  22.5 5.8 %all_gather.11 = f32[1,4,128,128]{3,2,0,1:T(8,128)S(1)} all-gather(f32[1,2,128,128]{3,2,0,1:T(8,128)S(1)} %bitcast.156), channel_id=1, replica_groups=mesh['shot'=2,'space'=128] {'shot'}, dimensions={1}, use_global_device_ids=true | all-gather | bytes 393216 | tf_op jit(solution)/shard_map/all_gather | solution.py:76
  28.2 5.6 %all_gather.10 = f32[1,4,128,128]{3,2,0,1:T(8,128)S(1)} all-gather(f32[1,2,128,128]{3,2,0,1:T(8,128)S(1)} %bitcast.157), channel_id=1, replica_groups=mesh['shot'=2,'space'=128] {'shot'}, dimensions={1}, use_global_device_ids=true | all-gather | bytes 393216 | tf_op jit(solution)/shard_map/all_gather | solution.py:75
  34.0 0.9 copy-done.8
  34.9 1.5 fusion.111
  37.0 0.6 scatter_fusion.1
  37.7 0.8 copy.31
  38.9 0.6 scatter_fusion
  39.6 1.0 copy-done.6
  40.8 8.4 %collective-permute-start.2 = (f32[2,4,128,128]{3,2,1,0:T(8,128)S(1)}, f32[2,4,128,128]{3,2,1,0:T(8,128)S(1)}, u32[]{:S(2)}, u32[]{:S(2)}) collective-permute-start(f32[2,4,128,128]{3,2,1,0:T(8,128)S(1)} %get-tuple-element.50), channel_id=1, source_target_pairs={{1,0},{2,1},{3,2},{4,3},{5,4},{6,5},{7,6},{8,7},{9,8},{10,9},{11,1... | collective-permute-start | bytes 1572872 | tf_op jit(solution)/shard_map/ppermute | solution.py:14
  49.2 1.9 collective-permute-start.3
  51.1 4.7 %collective-permute-done.2 = f32[2,4,128,128]{3,2,1,0:T(8,128)S(1)} collective-permute-done((f32[2,4,128,128]{3,2,1,0:T(8,128)S(1)}, f32[2,4,128,128]{3,2,1,0:T(8,128)S(1)}, u32[]{:S(2)}, u32[]{:S(2)}) %collective-permute-start.2) | collective-permute-done | bytes 524320 | tf_op jit(solution)/shard_map/ppermute | solution.py:14
  55.9 9.5 %collective-permute-done.3 = f32[2,4,128,128]{3,2,1,0:T(8,128)S(1)} collective-permute-done((f32[2,4,128,128]{3,2,1,0:T(8,128)S(1)}, f32[2,4,128,128]{3,2,1,0:T(8,128)S(1)}, u32[]{:S(2)}, u32[]{:S(2)}) %collective-permute-start.3) | collective-permute-done | bytes 524320 | tf_op jit(solution)/shard_map/ppermute | solution.py:14
  65.4 2.1 multiply_add_fusion.5
  68.1 0.6 scatter_fusion.3
  68.8 0.8 copy.35
  70.4 0.6 scatter_fusion.2
  71.1 1.0 copy-done.7
  72.2 1.9 collective-permute-start.4
  74.2 2.4 collective-permute-start.5
  76.6 4.3 collective-permute-done.4
  80.8 9.5 %collective-permute-done.5 = f32[2,4,128,128]{3,2,1,0:T(8,128)S(1)} collective-permute-done((f32[2,4,128,128]{3,2,1,0:T(8,128)S(1)}, f32[2,4,128,128]{3,2,1,0:T(8,128)S(1)}, u32[]{:S(2)}, u32[]{:S(2)}) %collective-permute-start.5) | collective-permute-done | bytes 524320 | tf_op jit(solution)/shard_map/ppermute | solution.py:14
  90.4 2.1 multiply_add_fusion.3
  93.1 0.6 scatter_fusion.5
  93.7 1.0 copy-done.4
  95.8 0.8 copy-done
  96.8 1.9 collective-permute-start.6
  98.7 2.6 collective-permute-start.7
  101.3 4.0 collective-permute-done.6
  105.4 9.5 %collective-permute-done.7 = f32[2,4,128,128]{3,2,1,0:T(8,128)S(1)} collective-permute-done((f32[2,4,128,128]{3,2,1,0:T(8,128)S(1)}, f32[2,4,128,128]{3,2,1,0:T(8,128)S(1)}, u32[]{:S(2)}, u32[]{:S(2)}) %collective-permute-start.7) | collective-permute-done | bytes 524320 | tf_op jit(solution)/shard_map/ppermute | solution.py:14
  114.9 2.1 multiply_add_fusion
  117.2 1.2 copy.54
  118.4 1.9 scatter_fusion.6
  120.3 2.0 broadcast_multiply_fusion.2
  122.2 4.8 %gather_fusion = f32[512]{0:T(512)S(1)} fusion(f32[2,65536]{1,0:T(2,128)S(1)} %get-tuple-element.39, s32[512]{0:T(512)S(1)} %bitcast.121), kind=kCustom, calls=%fused_computation.clone | custom fusion | bytes 8192 | tf_op jit(solution)/shard_map/jit(take_along_axis)/gather | solution.py:103
  127.1 4.8 %gather_fusion.1 = f32[512]{0:T(512)S(1)} fusion(f32[2,65536]{1,0:T(2,128)S(1)} %get-tuple-element.36, s32[512]{0:T(512)S(1)} %bitcast.122), kind=kCustom, calls=%fused_computation.1.clone | custom fusion | bytes 8192 | tf_op jit(solution)/shard_map/jit(take_along_axis)/gather | solution.py:103
  132.0 4.8 %gather_fusion.2 = f32[512]{0:T(512)S(1)} fusion(f32[2,65536]{1,0:T(2,128)S(1)} %get-tuple-element.37, s32[512]{0:T(512)S(1)} %bitcast.123), kind=kCustom, calls=%fused_computation.2.clone | custom fusion | bytes 8192 | tf_op jit(solution)/shard_map/jit(take_along_axis)/gather | solution.py:103
  136.8 4.8 %gather_fusion.3 = f32[512]{0:T(512)S(1)} fusion(f32[2,65536]{1,0:T(2,128)S(1)} %get-tuple-element.38, s32[512]{0:T(512)S(1)} %bitcast.124), kind=kCustom, calls=%fused_computation.3.clone | custom fusion | bytes 8192 | tf_op jit(solution)/shard_map/jit(take_along_axis)/gather | solution.py:103
  141.8 327.8 %psum.7 = f32[2,4,256]{2,0,1:T(2,128)S(1)} all-reduce(f32[2,4,256]{2,0,1:T(2,128)S(1)} %pad_maximum_fusion.8), channel_id=1, replica_groups=mesh['shot'=2,'space'=128] {'space'}, use_global_device_ids=true, to_apply=%region_8.10 | all-reduce | flops 2048 | bytes 16384 | tf_op jit(solution)/shard_map/psum | solution.py:107
  470.2 1.1 copy.41
  472.5 1.1 bitcast_multiply_fusion
  (66 shorter events, 7.1 us)
Async XLA Ops:
  0.6 0.7 copy-start.13
  1.5 0.7 copy-start.15
  2.2 0.7 copy-start.16
  2.9 9.7 %copy-start.10 = (f32[1,2,128,128]{3,2,1,0:T(8,128)S(1)}, f32[1,2,128,128]{3,2,1,0:T(8,128)}, u32[]{:S(2)}) copy-start(f32[1,2,128,128]{3,2,1,0:T(8,128)} %param.17) | copy-start | bytes 393220
  4.3 29.7 %collective-permute-start = (f32[2,4,128,128]{3,2,1,0:T(8,128)S(1)}, f32[2,4,128,128]{3,2,1,0:T(8,128)S(1)}, u32[]{:S(2)}, u32[]{:S(2)}) collective-permute-start(f32[2,4,128,128]{3,2,1,0:T(8,128)S(1)} %get-tuple-element.52), channel_id=1, source_target_pairs={{1,0},{2,1},{3,2},{4,3},{5,4},{6,5},{7,6},{8,7},{9,8},{10,9},{11,1... | collective-permute-start | bytes 1572872 | tf_op jit(solution)/shard_map/ppermute | solution.py:14
  10.7 23.3 %collective-permute-start.1 = (f32[2,4,128,128]{3,2,1,0:T(8,128)S(1)}, f32[2,4,128,128]{3,2,1,0:T(8,128)S(1)}, u32[]{:S(2)}, u32[]{:S(2)}) collective-permute-start(f32[2,4,128,128]{3,2,1,0:T(8,128)S(1)} %get-tuple-element.52), channel_id=1, source_target_pairs={{0,1},{1,2},{2,3},{3,4},{4,5},{5,6},{6,7},{7,8},{8,9},{9,10},{10,1... | collective-permute-start | bytes 1572872 | tf_op jit(solution)/shard_map/ppermute | solution.py:14
  21.5 0.9 copy-start.11
  22.5 5.8 %copy-start.12 = (f32[1,2,128,128]{3,2,1,0:T(8,128)S(1)}, f32[1,2,128,128]{3,2,1,0:T(8,128)}, u32[]{:S(2)}) copy-start(f32[1,2,128,128]{3,2,1,0:T(8,128)} %param.18) | copy-start | bytes 393220
  33.9 1.0 copy-start.8
  34.9 1.5 copy-start.9
  39.5 1.0 copy-start.6
  40.8 15.1 %collective-permute-start.2 = (f32[2,4,128,128]{3,2,1,0:T(8,128)S(1)}, f32[2,4,128,128]{3,2,1,0:T(8,128)S(1)}, u32[]{:S(2)}, u32[]{:S(2)}) collective-permute-start(f32[2,4,128,128]{3,2,1,0:T(8,128)S(1)} %get-tuple-element.50), channel_id=1, source_target_pairs={{1,0},{2,1},{3,2},{4,3},{5,4},{6,5},{7,6},{8,7},{9,8},{10,9},{11,1... | collective-permute-start | bytes 1572872 | tf_op jit(solution)/shard_map/ppermute | solution.py:14
  49.2 16.2 %collective-permute-start.3 = (f32[2,4,128,128]{3,2,1,0:T(8,128)S(1)}, f32[2,4,128,128]{3,2,1,0:T(8,128)S(1)}, u32[]{:S(2)}, u32[]{:S(2)}) collective-permute-start(f32[2,4,128,128]{3,2,1,0:T(8,128)S(1)} %get-tuple-element.50), channel_id=1, source_target_pairs={{0,1},{1,2},{2,3},{3,4},{4,5},{5,6},{6,7},{7,8},{8,9},{9,10},{10,1... | collective-permute-start | bytes 1572872 | tf_op jit(solution)/shard_map/ppermute | solution.py:14
  68.7 1.2 copy-start.5
  71.0 1.0 copy-start.7
  72.2 20.2 %copy-start.1 = (f32[2,4,128,128]{3,2,1,0:T(8,128)}, f32[2,4,128,128]{3,2,1,0:T(8,128)S(1)}, u32[]{:S(2)}) copy-start(f32[2,4,128,128]{3,2,1,0:T(8,128)S(1)} %get-tuple-element.47) | copy-start | bytes 1572868
  72.2 8.6 %collective-permute-start.4 = (f32[2,4,128,128]{3,2,1,0:T(8,128)S(1)}, f32[2,4,128,128]{3,2,1,0:T(8,128)S(1)}, u32[]{:S(2)}, u32[]{:S(2)}) collective-permute-start(f32[2,4,128,128]{3,2,1,0:T(8,128)S(1)} %get-tuple-element.47), channel_id=1, source_target_pairs={{1,0},{2,1},{3,2},{4,3},{5,4},{6,5},{7,6},{8,7},{9,8},{10,9},{11,1... | collective-permute-start | bytes 1572872 | tf_op jit(solution)/shard_map/ppermute | solution.py:14
  74.2 16.2 %collective-permute-start.5 = (f32[2,4,128,128]{3,2,1,0:T(8,128)S(1)}, f32[2,4,128,128]{3,2,1,0:T(8,128)S(1)}, u32[]{:S(2)}, u32[]{:S(2)}) collective-permute-start(f32[2,4,128,128]{3,2,1,0:T(8,128)S(1)} %get-tuple-element.47), channel_id=1, source_target_pairs={{0,1},{1,2},{2,3},{3,4},{4,5},{5,6},{6,7},{7,8},{8,9},{9,10},{10,1... | collective-permute-start | bytes 1572872 | tf_op jit(solution)/shard_map/ppermute | solution.py:14
  93.7 1.0 copy-start.4
  95.8 0.8 copy-start
  96.6 4.7 copy-start.14
  96.8 8.6 %collective-permute-start.6 = (f32[2,4,128,128]{3,2,1,0:T(8,128)S(1)}, f32[2,4,128,128]{3,2,1,0:T(8,128)S(1)}, u32[]{:S(2)}, u32[]{:S(2)}) collective-permute-start(f32[2,4,128,128]{3,2,1,0:T(8,128)S(1)} %get-tuple-element.42), channel_id=1, source_target_pairs={{1,0},{2,1},{3,2},{4,3},{5,4},{6,5},{7,6},{8,7},{9,8},{10,9},{11,1... | collective-permute-start | bytes 1572872 | tf_op jit(solution)/shard_map/ppermute | solution.py:14
  98.7 16.2 %collective-permute-start.7 = (f32[2,4,128,128]{3,2,1,0:T(8,128)S(1)}, f32[2,4,128,128]{3,2,1,0:T(8,128)S(1)}, u32[]{:S(2)}, u32[]{:S(2)}) collective-permute-start(f32[2,4,128,128]{3,2,1,0:T(8,128)S(1)} %get-tuple-element.42), channel_id=1, source_target_pairs={{0,1},{1,2},{2,3},{3,4},{4,5},{5,6},{6,7},{7,8},{8,9},{9,10},{10,1... | collective-permute-start | bytes 1572872 | tf_op jit(solution)/shard_map/ppermute | solution.py:14
  114.9 2.1 copy-start.2
  470.2 1.2 copy-start.3
where the time goes:
time: 474 us
  blocking collectives  348 us (73%)
  waiting for transfers between devices  41.7 us (9%)
  local copies, waits for them, and re-layouts  35.2 us (7%)
  starting transfers between devices  27.5 us (6%)
  other arithmetic  20 us (4%)
    psum x1, blocking collectives, per_device(): traces = lax.psum(local_traces, 'space')  328 us
    ppermute x8, waiting for transfers between devices, passed_along(): return lax.ppermute(value, axis, pairs)  41.7 us
    ppermute x8, starting transfers between devices, passed_along(): return lax.ppermute(value, axis, pairs)  27.5 us
    gather x8, local copies, waits for them, and re-layouts, per_device(): jnp.take_along_axis(new_p.reshape(stop - start, cells), receiver_local, a...  19.4 us
    unnamed x52, local copies, waits for them, and re-layouts  15.6 us
  transfers between devices with their start and end apart: 8, of which 6 were waited for; matrix products, arithmetic and copies ran while one was open for 0% of the time, Pallas kernels for 0%

commit v1 on v0

--- a/solution.py
+++ b/solution.py
@@ -1,3 +1,4 @@
+import functools
 import jax
 import jax.numpy as jnp
 from jax import lax
@@ -6,6 +7,14 @@
 STEPS = 4
 stencil_taps = (-205.0 / 72.0, 8.0 / 5.0, -1.0 / 5.0, 8.0 / 315.0, -1.0 / 560.0)
 step_ratio = 0.08
+
+
+def divide_the_group(block_in, link_axis):
+    then = jax.lax.all_gather(block_in, link_axis)
+    return jnp.sum(then, axis=0)
+
+
+shifts_all_run = functools.partial(divide_the_group, link_axis="space")
 
 
 def passed_along(value, axis, by):
@@ -104,7 +113,7 @@
         recorded[0].append(sampled * receiver_here)
         states[0] = (new_p, state[0], new_q, state[2])
     local_traces = jnp.concatenate([jnp.stack(samples, axis=1) for samples in recorded], axis=0)
-    traces = lax.psum(local_traces, "space")
+    traces = shifts_all_run(local_traces)
     pressure_final = jnp.concatenate([state[0] for state in states], axis=0).reshape(
         shots, 1, rows_x, rows_y, rows_z
     )

time: 474 us -> 263 us (0.55)
  the two profiles are of different devices: /device:TPU:128 before, /device:TPU:1 now
where the time goes in v1:
time: 263 us; the launch traced here: 262 us
  waiting for transfers between devices  141 us (54%)
  local copies, waits for them, and re-layouts  35.6 us (14%)
  starting transfers between devices  26.5 us (10%)
  other arithmetic  23.5 us (9%)
  blocking collectives  20.9 us (8%)
  between operations  14.4 us (5%)
    all_gather x1, waiting for transfers between devices, divide_the_group(): then = jax.lax.all_gather(block_in, link_axis)  123 us
    ppermute x8, starting transfers between devices, passed_along(): return lax.ppermute(value, axis, pairs)  26.5 us
    gather x8, local copies, waits for them, and re-layouts, per_device(): jnp.take_along_axis(new_p.reshape(stop - start, cells), receiver_local, a...  19.4 us
    ppermute x8, waiting for transfers between devices, passed_along(): return lax.ppermute(value, axis, pairs)  18.1 us
    unnamed x59, local copies, waits for them, and re-layouts  16 us
    all_gather x1, blocking collectives, per_device(): lax.all_gather(velocity, 'shot', axis=1, tiled=True)  11.3 us
    add x4, other arithmetic, advance(): 2.0 * pressure - pressure_prev  6.62 us
  transfers between devices with their start and end apart: 9, of which 7 were waited for; matrix products, arithmetic and copies ran while one was open for 1% of the time, Pallas kernels for 0%

profile of v1, /device:TPU:1, one launch (start us, length us, event | category | flops | bytes accessed | tf_op | source)
XLA Modules:
  0.0 262.3 jit_solution(14945224594272961078)
XLA Ops:
  8.1 0.6 copy-done.19
  8.7 0.6 copy-done.20
  9.4 1.4 bitcast_multiply_fusion.3
  10.8 5.1 %collective-permute-start = (f32[2,4,128,128]{3,2,1,0:T(8,128)S(1)}, f32[2,4,128,128]{3,2,1,0:T(8,128)S(1)}, u32[]{:S(2)}, u32[]{:S(2)}) collective-permute-start(f32[2,4,128,128]{3,2,1,0:T(8,128)S(1)} %get-tuple-element.49), channel_id=1, source_target_pairs={{1,0},{2,1},{3,2},{4,3},{5,4},{6,5},{7,6},{8,7},{9,8},{10,9},{11,1... | collective-permute-start | bytes 1572872 | tf_op jit(solution)/shard_map/ppermute | solution.py:23
  16.0 1.9 collective-permute-start.1
  17.9 11.3 %all_gather.15 = f32[1,4,128,128]{3,2,0,1:T(8,128)S(1)} all-gather(f32[1,2,128,128]{3,2,0,1:T(8,128)S(1)} %bitcast.155), channel_id=1, replica_groups=mesh['shot'=2,'space'=128] {'shot'}, dimensions={1}, use_global_device_ids=true | all-gather | bytes 393216 | tf_op jit(solution)/shard_map/all_gather | solution.py:83
  29.2 0.9 copy-done.15
  30.1 4.6 %all_gather.17 = f32[1,4,128,128]{3,2,0,1:T(8,128)S(1)} all-gather(f32[1,2,128,128]{3,2,0,1:T(8,128)S(1)} %bitcast.156), channel_id=1, replica_groups=mesh['shot'=2,'space'=128] {'shot'}, dimensions={1}, use_global_device_ids=true | all-gather | bytes 393216 | tf_op jit(solution)/shard_map/all_gather | solution.py:85
  34.7 5.0 %all_gather.16 = f32[1,4,128,128]{3,2,0,1:T(8,128)S(1)} all-gather(f32[1,2,128,128]{3,2,0,1:T(8,128)S(1)} %bitcast.157), channel_id=1, replica_groups=mesh['shot'=2,'space'=128] {'shot'}, dimensions={1}, use_global_device_ids=true | all-gather | bytes 393216 | tf_op jit(solution)/shard_map/all_gather | solution.py:84
  39.8 0.9 copy-done.12
  40.8 2.1 fusion.111
  43.5 0.6 scatter_fusion.1
  44.2 0.8 copy.32
  45.8 0.6 scatter_fusion
  46.5 1.0 copy-done.9
  47.6 4.7 %collective-permute-start.2 = (f32[2,4,128,128]{3,2,1,0:T(8,128)S(1)}, f32[2,4,128,128]{3,2,1,0:T(8,128)S(1)}, u32[]{:S(2)}, u32[]{:S(2)}) collective-permute-start(f32[2,4,128,128]{3,2,1,0:T(8,128)S(1)} %get-tuple-element.47), channel_id=1, source_target_pairs={{1,0},{2,1},{3,2},{4,3},{5,4},{6,5},{7,6},{8,7},{9,8},{10,9},{11,1... | collective-permute-start | bytes 1572872 | tf_op jit(solution)/shard_map/ppermute | solution.py:23
  52.3 1.9 collective-permute-start.3
  54.2 3.9 %collective-permute-done.2 = f32[2,4,128,128]{3,2,1,0:T(8,128)S(1)} collective-permute-done((f32[2,4,128,128]{3,2,1,0:T(8,128)S(1)}, f32[2,4,128,128]{3,2,1,0:T(8,128)S(1)}, u32[]{:S(2)}, u32[]{:S(2)}) %collective-permute-start.2) | collective-permute-done | bytes 524320 | tf_op jit(solution)/shard_map/ppermute | solution.py:23
  58.1 2.2 collective-permute-done.3
  60.3 2.1 multiply_add_fusion.5
  63.7 0.8 copy.36
  65.4 0.6 scatter_fusion.2
  66.0 1.0 copy-done.10
  67.2 1.9 collective-permute-start.4
  69.1 4.4 %collective-permute-start.5 = (f32[2,4,128,128]{3,2,1,0:T(8,128)S(1)}, f32[2,4,128,128]{3,2,1,0:T(8,128)S(1)}, u32[]{:S(2)}, u32[]{:S(2)}) collective-permute-start(f32[2,4,128,128]{3,2,1,0:T(8,128)S(1)} %get-tuple-element.44), channel_id=1, source_target_pairs={{0,1},{1,2},{2,3},{3,4},{4,5},{5,6},{6,7},{7,8},{8,9},{9,10},{10,1... | collective-permute-start | bytes 1572872 | tf_op jit(solution)/shard_map/ppermute | solution.py:23
  73.5 4.9 %collective-permute-done.4 = f32[2,4,128,128]{3,2,1,0:T(8,128)S(1)} collective-permute-done((f32[2,4,128,128]{3,2,1,0:T(8,128)S(1)}, f32[2,4,128,128]{3,2,1,0:T(8,128)S(1)}, u32[]{:S(2)}, u32[]{:S(2)}) %collective-permute-start.4) | collective-permute-done | bytes 524320 | tf_op jit(solution)/shard_map/ppermute | solution.py:23
  78.5 1.2 collective-permute-done.5
  79.6 2.1 multiply_add_fusion.3
  82.4 0.6 scatter_fusion.5
  83.0 0.8 copy.40
  84.7 0.6 scatter_fusion.4
  85.4 1.2 copy-done.11
  86.7 1.9 collective-permute-start.6
  88.7 4.6 %collective-permute-start.7 = (f32[2,4,128,128]{3,2,1,0:T(8,128)S(1)}, f32[2,4,128,128]{3,2,1,0:T(8,128)S(1)}, u32[]{:S(2)}, u32[]{:S(2)}) collective-permute-start(f32[2,4,128,128]{3,2,1,0:T(8,128)S(1)} %get-tuple-element.39), channel_id=1, source_target_pairs={{0,1},{1,2},{2,3},{3,4},{4,5},{5,6},{6,7},{7,8},{8,9},{9,10},{10,1... | collective-permute-start | bytes 1572872 | tf_op jit(solution)/shard_map/ppermute | solution.py:23
  93.3 4.7 %collective-permute-done.6 = f32[2,4,128,128]{3,2,1,0:T(8,128)S(1)} collective-permute-done((f32[2,4,128,128]{3,2,1,0:T(8,128)S(1)}, f32[2,4,128,128]{3,2,1,0:T(8,128)S(1)}, u32[]{:S(2)}, u32[]{:S(2)}) %collective-permute-start.6) | collective-permute-done | bytes 524320 | tf_op jit(solution)/shard_map/ppermute | solution.py:23
  98.0 1.2 collective-permute-done.7
  99.2 2.1 multiply_add_fusion
  101.5 1.2 copy.55
  102.7 1.9 scatter_fusion.6
  104.6 2.0 broadcast_multiply_fusion.2
  106.5 4.8 %gather_fusion = f32[512]{0:T(512)S(1)} fusion(f32[2,65536]{1,0:T(2,128)S(1)} %get-tuple-element.36, s32[512]{0:T(512)S(1)} %bitcast.120), kind=kCustom, calls=%fused_computation.clone | custom fusion | bytes 8192 | tf_op jit(solution)/shard_map/jit(take_along_axis)/gather | solution.py:112
  111.4 4.8 %gather_fusion.1 = f32[512]{0:T(512)S(1)} fusion(f32[2,65536]{1,0:T(2,128)S(1)} %get-tuple-element.33, s32[512]{0:T(512)S(1)} %bitcast.121), kind=kCustom, calls=%fused_computation.1.clone | custom fusion | bytes 8192 | tf_op jit(solution)/shard_map/jit(take_along_axis)/gather | solution.py:112
  116.3 4.8 %gather_fusion.2 = f32[512]{0:T(512)S(1)} fusion(f32[2,65536]{1,0:T(2,128)S(1)} %get-tuple-element.34, s32[512]{0:T(512)S(1)} %bitcast.122), kind=kCustom, calls=%fused_computation.2.clone | custom fusion | bytes 8192 | tf_op jit(solution)/shard_map/jit(take_along_axis)/gather | solution.py:112
  121.1 4.8 %gather_fusion.3 = f32[512]{0:T(512)S(1)} fusion(f32[2,65536]{1,0:T(2,128)S(1)} %get-tuple-element.35, s32[512]{0:T(512)S(1)} %bitcast.123), kind=kCustom, calls=%fused_computation.3.clone | custom fusion | bytes 8192 | tf_op jit(solution)/shard_map/jit(take_along_axis)/gather | solution.py:112
  126.7 1.1 copy.42
  129.0 1.1 bitcast_multiply_fusion
  130.1 123.3 %all-gather.3.cloned.1.call-done = f32[256,4,256]{2,1,0:T(4,128)} async-done(((f32[2,4,256]{2,1,0:T(4,128)}), f32[256,4,256]{2,1,0:T(4,128)}) %all-gather.3.cloned.1.call-update) | async-done | bytes 1048592 | tf_op jit(solution)/shard_map/all_gather | solution.py:13
  253.4 2.0 reduce_sum.9
  (80 shorter events, 8.7 us)
Async XLA Ops:
  7.2 0.7 copy-start.17
  7.2 246.3 %all-gather.3.cloned.1.call-start = ((), (), s32[]{:S(2)}) async-start(), calls=%async_computation | async-start | bytes 1056768 | tf_op jit(solution)/shard_map/all_gather | solution.py:13
  8.1 0.7 copy-start.19
  8.7 0.7 copy-start.20
  9.4 8.5 %copy-start.14 = (f32[1,2,128,128]{3,2,1,0:T(8,128)S(1)}, f32[1,2,128,128]{3,2,1,0:T(8,128)}, u32[]{:S(2)}) copy-start(f32[1,2,128,128]{3,2,1,0:T(8,128)} %param.17) | copy-start | bytes 393220
  10.8 29.0 %collective-permute-start = (f32[2,4,128,128]{3,2,1,0:T(8,128)S(1)}, f32[2,4,128,128]{3,2,1,0:T(8,128)S(1)}, u32[]{:S(2)}, u32[]{:S(2)}) collective-permute-start(f32[2,4,128,128]{3,2,1,0:T(8,128)S(1)} %get-tuple-element.49), channel_id=1, source_target_pairs={{1,0},{2,1},{3,2},{4,3},{5,4},{6,5},{7,6},{8,7},{9,8},{10,9},{11,1... | collective-permute-start | bytes 1572872 | tf_op jit(solution)/shard_map/ppermute | solution.py:23
  16.0 23.9 %collective-permute-start.1 = (f32[2,4,128,128]{3,2,1,0:T(8,128)S(1)}, f32[2,4,128,128]{3,2,1,0:T(8,128)S(1)}, u32[]{:S(2)}, u32[]{:S(2)}) collective-permute-start(f32[2,4,128,128]{3,2,1,0:T(8,128)S(1)} %get-tuple-element.49), channel_id=1, source_target_pairs={{0,1},{1,2},{2,3},{3,4},{4,5},{5,6},{6,7},{7,8},{8,9},{9,10},{10,1... | collective-permute-start | bytes 1572872 | tf_op jit(solution)/shard_map/ppermute | solution.py:23
  29.2 0.9 copy-start.15
  30.1 4.6 %copy-start.16 = (f32[1,2,128,128]{3,2,1,0:T(8,128)S(1)}, f32[1,2,128,128]{3,2,1,0:T(8,128)}, u32[]{:S(2)}) copy-start(f32[1,2,128,128]{3,2,1,0:T(8,128)} %param.18) | copy-start | bytes 393220
  39.7 1.0 copy-start.12
  40.7 2.2 copy-start.13
  44.2 1.2 copy-start.8
  46.4 1.0 copy-start.9
  47.6 14.8 %copy-start.1 = (f32[2,4,128,128]{3,2,1,0:T(8,128)}, f32[2,4,128,128]{3,2,1,0:T(8,128)S(1)}, u32[]{:S(2)}) copy-start(f32[2,4,128,128]{3,2,1,0:T(8,128)S(1)} %get-tuple-element.47) | copy-start | bytes 1572868
  47.6 10.5 %collective-permute-start.2 = (f32[2,4,128,128]{3,2,1,0:T(8,128)S(1)}, f32[2,4,128,128]{3,2,1,0:T(8,128)S(1)}, u32[]{:S(2)}, u32[]{:S(2)}) collective-permute-start(f32[2,4,128,128]{3,2,1,0:T(8,128)S(1)} %get-tuple-element.47), channel_id=1, source_target_pairs={{1,0},{2,1},{3,2},{4,3},{5,4},{6,5},{7,6},{8,7},{9,8},{10,9},{11,1... | collective-permute-start | bytes 1572872 | tf_op jit(solution)/shard_map/ppermute | solution.py:23
  52.3 8.0 %collective-permute-start.3 = (f32[2,4,128,128]{3,2,1,0:T(8,128)S(1)}, f32[2,4,128,128]{3,2,1,0:T(8,128)S(1)}, u32[]{:S(2)}, u32[]{:S(2)}) collective-permute-start(f32[2,4,128,128]{3,2,1,0:T(8,128)S(1)} %get-tuple-element.47), channel_id=1, source_target_pairs={{0,1},{1,2},{2,3},{3,4},{4,5},{5,6},{6,7},{7,8},{8,9},{9,10},{10,1... | collective-permute-start | bytes 1572872 | tf_op jit(solution)/shard_map/ppermute | solution.py:23
  63.7 1.2 copy-start.7
  66.0 1.0 copy-start.10
  67.0 12.6 %copy-start.2 = (f32[2,4,128,128]{3,2,1,0:T(8,128)S(1)}, f32[2,4,128,128]{3,2,1,0:T(8,128)}, u32[]{:S(2)}) copy-start(f32[2,4,128,128]{3,2,1,0:T(8,128)} %copy-done.1) | copy-start | bytes 1572868
  67.2 14.6 %copy-start.3 = (f32[2,4,128,128]{3,2,1,0:T(8,128)}, f32[2,4,128,128]{3,2,1,0:T(8,128)S(1)}, u32[]{:S(2)}) copy-start(f32[2,4,128,128]{3,2,1,0:T(8,128)S(1)} %get-tuple-element.44) | copy-start | bytes 1572868
  67.2 11.2 %collective-permute-start.4 = (f32[2,4,128,128]{3,2,1,0:T(8,128)S(1)}, f32[2,4,128,128]{3,2,1,0:T(8,128)S(1)}, u32[]{:S(2)}, u32[]{:S(2)}) collective-permute-start(f32[2,4,128,128]{3,2,1,0:T(8,128)S(1)} %get-tuple-element.44), channel_id=1, source_target_pairs={{1,0},{2,1},{3,2},{4,3},{5,4},{6,5},{7,6},{8,7},{9,8},{10,9},{11,1... | collective-permute-start | bytes 1572872 | tf_op jit(solution)/shard_map/ppermute | solution.py:23
  69.1 10.5 %collective-permute-start.5 = (f32[2,4,128,128]{3,2,1,0:T(8,128)S(1)}, f32[2,4,128,128]{3,2,1,0:T(8,128)S(1)}, u32[]{:S(2)}, u32[]{:S(2)}) collective-permute-start(f32[2,4,128,128]{3,2,1,0:T(8,128)S(1)} %get-tuple-element.44), channel_id=1, source_target_pairs={{0,1},{1,2},{2,3},{3,4},{4,5},{5,6},{6,7},{7,8},{8,9},{9,10},{10,1... | collective-permute-start | bytes 1572872 | tf_op jit(solution)/shard_map/ppermute | solution.py:23
  83.0 1.2 copy-start.6
  85.3 1.4 copy-start
  85.3 1.2 copy-start.11
  86.5 6.7 %copy-start.18 = (s32[2,256]{1,0:T(2,128)S(1)}, s32[2,256]{1,0:T(2,128)}, u32[]{:S(2)}) copy-start(s32[2,256]{1,0:T(2,128)} %param.22) | copy-start | bytes 6148
  86.7 11.2 %collective-permute-start.6 = (f32[2,4,128,128]{3,2,1,0:T(8,128)S(1)}, f32[2,4,128,128]{3,2,1,0:T(8,128)S(1)}, u32[]{:S(2)}, u32[]{:S(2)}) collective-permute-start(f32[2,4,128,128]{3,2,1,0:T(8,128)S(1)} %get-tuple-element.39), channel_id=1, source_target_pairs={{1,0},{2,1},{3,2},{4,3},{5,4},{6,5},{7,6},{8,7},{9,8},{10,9},{11,1... | collective-permute-start | bytes 1572872 | tf_op jit(solution)/shard_map/ppermute | solution.py:23
  88.7 10.5 %collective-permute-start.7 = (f32[2,4,128,128]{3,2,1,0:T(8,128)S(1)}, f32[2,4,128,128]{3,2,1,0:T(8,128)S(1)}, u32[]{:S(2)}, u32[]{:S(2)}) collective-permute-start(f32[2,4,128,128]{3,2,1,0:T(8,128)S(1)} %get-tuple-element.39), channel_id=1, source_target_pairs={{0,1},{1,2},{2,3},{3,4},{4,5},{5,6},{6,7},{7,8},{8,9},{9,10},{10,1... | collective-permute-start | bytes 1572872 | tf_op jit(solution)/shard_map/ppermute | solution.py:23
  99.2 2.1 copy-start.4
  126.7 1.2 copy-start.5
Sparse Core Ops, SparseCore 0:
  126.8 126.5 all-gather.2
